TPU v7x, 256 devices: a whole 4x4x8 slice. The times are simulated.
256 devices in a mesh: row: 32 (over x, y, core), col: 8 (over z).
Axes of the slice: x: 4, y: 4, z: 8, core: 2. Of those that a mesh axis runs over, the one named last changes fastest.
Arguments:
- test_kernel: float32 [65536, 4096], P('row', 'col'), may hold values from -6 to 6
- first_panel: float32 [65536, 512], P('row', 'col'), may hold values from -0.25 to 0.25
- second_panel: float32 [65536, 512], P('row', 'col'), may hold values from -0.25 to 0.25
- first_inverse: float32 [512, 512], replicated, may hold values from -0.15 to 1.5, as said below
- second_inverse: float32 [512, 512], replicated, may hold values from -0.15 to 1.5, as said below
Outputs:
- solution: float32 [65536, 4096], P('row', 'col')
Inputs may be any that keep to these rules, and one draw needn't show every extreme that they name: `first_inverse`: lower triangular: zeros above the diagonal, diagonal entries positive. `second_inverse`: lower triangular: zeros above the diagonal, diagonal entries positive.
All inputs are finite; a program needn't handle non-finite values.
Results may differ from a plain program's by a relative error of at most 0.000075.
Values sent between devices are 32-bit elements; how exact they have to be, the bound alone decides.
A program may use at most 64 MiB of HBM per device.

v0:
```python
import jax
import jax.numpy as jnp
from jax import lax
from jax.sharding import PartitionSpec as P


def broadcast(value, axis, source):
    kept = jnp.where(lax.axis_index(axis) == source, value, 0).astype(value.dtype)
    return lax.psum(kept, axis)


def product(left, right):
    return jnp.dot(left, right, precision=lax.Precision.HIGHEST, preferred_element_type=jnp.float32)


def folding(solved, piece):
    return product(piece, solved)


def per_device(test_kernel, first_panel, second_panel, first_inverse, second_inverse):
    block = first_inverse.shape[0]
    position = lax.axis_index("row")
    first_rows = broadcast(test_kernel[:block], "row", 0)
    first_solved = product(first_inverse, first_rows)
    update_one = folding(first_solved, lax.all_gather(first_panel, "col", axis=1, tiled=True))
    partial_value = test_kernel - update_one
    second_rows = broadcast(partial_value[:block], "row", 1)
    second_solved = product(second_inverse, second_rows)
    update_two = folding(second_solved, lax.all_gather(second_panel, "col", axis=1, tiled=True))
    final = partial_value - update_two
    leading_final = jnp.where(
        position == 0, first_solved, jnp.where(position == 1, second_solved, final[:block])
    )
    return final.at[:block].set(leading_final)


def solution(mesh):
    in_specs = (P("row", "col"), P("row", "col"), P("row", "col"), P(), P())
    out_specs = P("row", "col")
    return jax.shard_map(
        per_device, mesh=mesh, in_specs=in_specs, out_specs=out_specs, check_vma=False
    )
```

profile of v0, /device:TPU:1, one launch (start us, length us, event | category | flops | bytes accessed | tf_op | source)
XLA Modules:
  0.0 296.1 jit_solution(15105920552222023866)
XLA Ops:
  7.4 0.0 copy-start
  7.4 0.0 all-reduce.3.cloned.1.call-start
  7.4 5.4 %copy.7 = f32[2048,512]{0,1:T(8,128)} copy(f32[2048,512]{1,0:T(8,128)} %param.7) | data formatting | bytes 8388608 | tf_op args[0]
  12.8 2.3 slice_select_fusion.2
  15.1 0.0 all-reduce.3.cloned.1.call-update
  15.1 0.0 all-gather.3.cloned.1.call-start
  15.2 0.5 all-gather.3.cloned.1.call-update
  15.7 0.0 all-reduce.5.cloned.1.call-start
  15.8 119.1 %all-reduce.3.cloned.1.call-done = f32[512,512]{0,1:T(8,128)} async-done(((f32[512,512]{0,1:T(8,128)}), f32[512,512]{0,1:T(8,128)}) %all-reduce.3.cloned.1.call-update) | async-done | bytes 1048592 | tf_op jit(solution)/shard_map/psum | solution.py:9
  134.9 0.0 copy-done
  134.9 3.1 %fusion.2 = f32[512,512]{1,0:T(8,128)S(1)} fusion(f32[512,512]{0,1:T(8,128)} %all-reduce.3.cloned.1.call-done, f32[512,512]{1,0:T(8,128)S(1)} %copy-done), kind=kOutput, calls=%fused_computation.7 | convolution fusion | flops 1610612736 | bytes 3145728 | tf_op jit(solution)/shard_map/dot_general | solution.py:13
  138.0 0.0 all-gather.3.cloned.1.call-done
  138.0 9.4 %bitcast_subtract_fusion.1 = f32[2048,512]{0,1:T(8,128)S(1)} fusion(f32[2048,512]{0,1:T(8,128)} %copy.7, f32[512,512]{1,0:T(8,128)S(1)} %fusion.2, f32[2048,512]{0,1:T(8,128)} %all-gather.3.cloned.1.call-done), kind=kOutput, calls=%fused_computation.1 | convolution fusion | flops 6443499520 | bytes 13631488 | tf_op jit(solution)/shard_map/dot_general | solution.py:13
  147.5 0.0 copy-start.1
  147.5 2.0 copy-done.1
  149.5 1.1 slice_select_fusion.1
  150.6 0.0 all-reduce.5.cloned.1.call-update
  150.6 0.2 all-gather.5.cloned.1.call-start
  150.9 0.4 all-gather.5.cloned.1.call-update
  151.2 115.2 %all-reduce.5.cloned.1.call-done = f32[512,512]{0,1:T(8,128)} async-done(((f32[512,512]{0,1:T(8,128)}), f32[512,512]{0,1:T(8,128)}) %all-reduce.5.cloned.1.call-update) | async-done | bytes 1048592 | tf_op jit(solution)/shard_map/psum | solution.py:9
  266.5 3.4 %fusion.3 = f32[512,512]{1,0:T(8,128)S(1)} fusion(f32[512,512]{0,1:T(8,128)} %all-reduce.5.cloned.1.call-done, f32[512,512]{1,0:T(8,128)} %param.11), kind=kOutput, calls=%fused_computation.8 | convolution fusion | flops 1610612736 | bytes 3145728 | tf_op jit(solution)/shard_map/dot_general | solution.py:13
  269.9 0.0 all-gather.5.cloned.1.call-done
  269.9 10.8 %bitcast_subtract_fusion = f32[2048,512]{0,1:T(8,128)} fusion(f32[2048,512]{0,1:T(8,128)} %copy-done.1, f32[512,512]{1,0:T(8,128)S(1)} %fusion.3, f32[2048,512]{0,1:T(8,128)} %all-gather.5.cloned.1.call-done), kind=kOutput, calls=%fused_computation | convolution fusion | flops 6443499520 | bytes 13631488 | tf_op jit(solution)/shard_map/dot_general | solution.py:13
  280.7 2.6 fusion.1
  283.3 5.3 %copy.8 = f32[2048,512]{1,0:T(8,128)} copy(f32[2048,512]{0,1:T(8,128)} %fusion.1) | data formatting | bytes 8388608 | tf_op jit(solution)/shard_map/scatter | solution.py:34
Async XLA Ops:
  7.4 127.6 %copy-start = (f32[512,512]{1,0:T(8,128)S(1)}, f32[512,512]{1,0:T(8,128)}, u32[]{:S(2)}) copy-start(f32[512,512]{1,0:T(8,128)} %param.10) | copy-start | bytes 3145732
  7.4 127.5 %all-reduce.3.cloned.1.call-start = ((), (), s32[]{:S(2)}) async-start(), calls=%async_computation | async-start | bytes 2097152 | tf_op jit(solution)/shard_map/psum | solution.py:9
  15.1 122.9 %all-gather.3.cloned.1.call-start = ((), (), s32[]{:S(2)}) async-start(), calls=%async_computation.1 | async-start | bytes 4718592 | tf_op jit(solution)/shard_map/all_gather | solution.py:25
  15.7 250.7 %all-reduce.5.cloned.1.call-start = ((), (), s32[]{:S(2)}) async-start(), calls=%async_computation.2 | async-start | bytes 2097152 | tf_op jit(solution)/shard_map/psum | solution.py:9
  147.5 2.0 copy-start.1
  150.6 119.3 %all-gather.5.cloned.1.call-start = ((), (), s32[]{:S(2)}) async-start(), calls=%async_computation.3 | async-start | bytes 4718592 | tf_op jit(solution)/shard_map/all_gather | solution.py:29
Sparse Core Ops, SparseCore 0:
  15.3 119.6 all-reduce.2
  150.8 115.6 all-reduce.4
Sparse Core Ops, SparseCore 1:
  17.5 58.4 all-gather.2
  152.9 54.4 all-gather.4
where the time goes:
time: 296 us
  waiting for transfers between devices  235 us (79%)
  matrix products  26.7 us (9%)
  between operations  14.9 us (5%)
  local copies, waits for them, and re-layouts  12.8 us (4%)
  other arithmetic  6.08 us (2%)
    psum x2, waiting for transfers between devices, broadcast(): return lax.psum(kept, axis)  234 us
    dot_general x4, matrix products, product(): jnp.dot(left, right, precision=lax.Precision.HIGHEST, preferred_element_t...  26.7 us
    unnamed x5, local copies, waits for them, and re-layouts  7.44 us
  transfers between devices with their start and end apart: 4, of which 2 were waited for; matrix products, arithmetic and copies ran while one was open for 2% of the time, Pallas kernels for 0%

commit v1 on v0

--- a/solution.py
+++ b/solution.py
@@ -6,7 +6,8 @@
 
 def broadcast(value, axis, source):
     kept = jnp.where(lax.axis_index(axis) == source, value, 0).astype(value.dtype)
-    return lax.psum(kept, axis)
+    report_the_leaves = lambda block_here, ax_name: lax.all_gather(block_here, ax_name).sum(axis=0)
+    return report_the_leaves(kept, axis)
 
 
 def product(left, right):

time: 296 us -> 405 us (1.37)
  local copies, waits for them, and re-layouts: 12.8 us -> 77.8 us
  waiting for transfers between devices: 235 us -> 272 us
  other arithmetic: 6.08 us -> 16.8 us
    all_gather x0 -> x2, waiting for transfers between devices: none -> 240 us  [broadcast(): lax.all_gather(block_here, ax_name).sum(axis=0)]
    psum x2 -> x0, waiting for transfers between devices: 234 us -> none  [broadcast(): return lax.psum(kept, axis)]
    unnamed x5 -> x11, local copies, waits for them, and re-layouts: 7.44 us -> 72.5 us
    all_gather x1, waiting for transfers between devices: 0.03 us -> 15.9 us  [per_device(): lax.all_gather(first_panel, 'col', axis=1, tiled=True)]
    all_gather x1, waiting for transfers between devices: 0.03 us -> 15.7 us  [per_device(): lax.all_gather(second_panel, 'col', axis=1, tiled=True)]
    reduce_sum x0 -> x2, other arithmetic: none -> 10.7 us  [broadcast(): lax.all_gather(block_here, ax_name).sum(axis=0)]
  transfers between devices with their start and end apart: 4 -> 4, of which waited for: 2 -> 4; matrix products, arithmetic and copies ran while one was open for 2% -> 20% of each run, Pallas kernels for 0% -> 0%
where the time goes in v1:
time: 405 us; the launch traced here: 404 us
  waiting for transfers between devices  272 us (67%)
  local copies, waits for them, and re-layouts  77.8 us (19%)
  matrix products  23.9 us (6%)
  other arithmetic  16.8 us (4%)
  between operations  13.2 us (3%)
    all_gather x2, waiting for transfers between devices, broadcast(): lax.all_gather(block_here, ax_name).sum(axis=0)  240 us
    unnamed x11, local copies, waits for them, and re-layouts  72.5 us
    dot_general x4, matrix products, product(): jnp.dot(left, right, precision=lax.Precision.HIGHEST, preferred_element_t...  23.9 us
    all_gather x1, waiting for transfers between devices, per_device(): lax.all_gather(first_panel, 'col', axis=1, tiled=True)  15.9 us
    all_gather x1, waiting for transfers between devices, per_device(): lax.all_gather(second_panel, 'col', axis=1, tiled=True)  15.7 us
    reduce_sum x2, other arithmetic, broadcast(): lax.all_gather(block_here, ax_name).sum(axis=0)  10.7 us
  transfers between devices with their start and end apart: 4, of which 4 were waited for; matrix products, arithmetic and copies ran while one was open for 20% of the time, Pallas kernels for 0%

profile of v1, /device:TPU:1, one launch (start us, length us, event | category | flops | bytes accessed | tf_op | source)
XLA Modules:
  0.0 404.4 jit_solution(6480048097025427625)
XLA Ops:
  6.5 0.0 copy-start
  6.5 0.0 all-gather.11.cloned.1.call-start
  6.5 5.4 %copy.10 = f32[2048,512]{0,1:T(8,128)} copy(f32[2048,512]{1,0:T(8,128)} %param.7) | data formatting | bytes 8388608 | tf_op args[0]
  12.0 2.3 slice_select_fusion.2
  14.3 0.0 all-gather.11.cloned.1.call-update
  14.3 0.0 all-gather.7.cloned.1.call-start
  14.3 0.7 all-gather.7.cloned.1.call-update
  15.0 0.0 all-gather.13.cloned.1.call-start
  15.1 122.4 %all-gather.11.cloned.1.call-done = f32[16384,512]{0,1:T(8,128)} async-done(((f32[512,512]{0,1:T(8,128)}), f32[16384,512]{0,1:T(8,128)}) %all-gather.11.cloned.1.call-update) | async-done | bytes 33554448 | tf_op jit(solution)/shard_map/all_gather | solution.py:9
  137.5 32.5 %copy.12 = f32[64,8,32,512]{3,2,1,0:T(8,128)S(1)} copy(f32[64,8,32,512]{3,1,2,0:T(8,128)} %bitcast.26) | data formatting | bytes 67108864
  170.0 5.4 %bitcast_reduce_fusion.1 = f32[512,512]{0,1:T(8,128)S(1)} fusion(f32[64,8,32,512]{3,2,1,0:T(8,128)S(1)} %copy.12), kind=kLoop, calls=%fused_computation.1 | loop fusion | flops 8126464 | bytes 34603008 | tf_op jit(solution)/shard_map/reduce_sum | solution.py:9
  175.3 0.0 copy-done
  175.4 1.9 fusion.2
  177.2 15.9 %all-gather.7.cloned.1.call-done = f32[2048,512]{0,1:T(8,128)} async-done(((f32[2048,64]{0,1:T(8,128)}), f32[2048,512]{0,1:T(8,128)}) %all-gather.7.cloned.1.call-update) | async-done | bytes 4194320 | tf_op jit(solution)/shard_map/all_gather | solution.py:26
  193.1 9.4 %bitcast_subtract_fusion.1 = f32[2048,512]{0,1:T(8,128)S(1)} fusion(f32[2048,512]{0,1:T(8,128)} %copy.10, f32[512,512]{1,0:T(8,128)S(1)} %fusion.2, f32[2048,512]{0,1:T(8,128)} %all-gather.7.cloned.1.call-done), kind=kOutput, calls=%fused_computation.3 | convolution fusion | flops 6443499520 | bytes 13631488 | tf_op jit(solution)/shard_map/dot_general | solution.py:14
  202.5 0.0 copy-start.2
  202.5 2.0 copy-done.2
  204.5 1.1 slice_select_fusion.1
  205.6 0.0 all-gather.13.cloned.1.call-update
  205.6 0.2 all-gather.9.cloned.1.call-start
  205.9 0.3 all-gather.9.cloned.1.call-update
  206.2 117.4 %all-gather.13.cloned.1.call-done = f32[16384,512]{0,1:T(8,128)} async-done(((f32[512,512]{0,1:T(8,128)}), f32[16384,512]{0,1:T(8,128)}) %all-gather.13.cloned.1.call-update) | async-done | bytes 33554448 | tf_op jit(solution)/shard_map/all_gather | solution.py:9
  323.6 32.5 %copy.13 = f32[64,8,32,512]{3,2,1,0:T(8,128)S(1)} copy(f32[64,8,32,512]{3,1,2,0:T(8,128)} %bitcast.27) | data formatting | bytes 67108864
  356.1 0.0 copy-start.3
  356.1 5.4 %bitcast_reduce_fusion = f32[512,512]{0,1:T(8,128)S(1)} fusion(f32[64,8,32,512]{3,2,1,0:T(8,128)S(1)} %copy.13), kind=kLoop, calls=%fused_computation | loop fusion | flops 8126464 | bytes 34603008 | tf_op jit(solution)/shard_map/reduce_sum | solution.py:9
  361.5 0.0 copy-done.3
  361.5 1.9 fusion.3
  363.4 15.7 %all-gather.9.cloned.1.call-done = f32[2048,512]{0,1:T(8,128)} async-done(((f32[2048,64]{0,1:T(8,128)}), f32[2048,512]{0,1:T(8,128)}) %all-gather.9.cloned.1.call-update) | async-done | bytes 4194320 | tf_op jit(solution)/shard_map/all_gather | solution.py:30
  379.1 10.8 %bitcast_subtract_fusion = f32[2048,512]{0,1:T(8,128)} fusion(f32[2048,512]{0,1:T(8,128)} %copy-done.2, f32[512,512]{1,0:T(8,128)S(1)} %fusion.3, f32[2048,512]{0,1:T(8,128)} %all-gather.9.cloned.1.call-done), kind=kOutput, calls=%fused_computation.2 | convolution fusion | flops 6443499520 | bytes 13631488 | tf_op jit(solution)/shard_map/dot_general | solution.py:14
  389.9 2.7 fusion.1
  392.6 5.3 %copy.11 = f32[2048,512]{1,0:T(8,128)} copy(f32[2048,512]{0,1:T(8,128)} %fusion.1) | data formatting | bytes 8388608 | tf_op jit(solution)/shard_map/scatter | solution.py:35
  397.9 0.0 copy-done.1
  (1 shorter events, 0.0 us)
Async XLA Ops:
  6.5 168.8 %copy-start = (f32[512,512]{1,0:T(8,128)S(1)}, f32[512,512]{1,0:T(8,128)}, u32[]{:S(2)}) copy-start(f32[512,512]{1,0:T(8,128)} %param.10) | copy-start | bytes 3145732
  6.5 130.9 %all-gather.11.cloned.1.call-start = ((), (), s32[]{:S(2)}) async-start(), calls=%async_computation.2 | async-start | bytes 34603008 | tf_op jit(solution)/shard_map/all_gather | solution.py:9
  14.3 178.8 %all-gather.7.cloned.1.call-start = ((), (), s32[]{:S(2)}) async-start(), calls=%async_computation | async-start | bytes 4718592 | tf_op jit(solution)/shard_map/all_gather | solution.py:26
  15.0 308.6 %all-gather.13.cloned.1.call-start = ((), (), s32[]{:S(2)}) async-start(), calls=%async_computation.3 | async-start | bytes 34603008 | tf_op jit(solution)/shard_map/all_gather | solution.py:9
  202.5 2.0 copy-start.2
  205.6 173.5 %all-gather.9.cloned.1.call-start = ((), (), s32[]{:S(2)}) async-start(), calls=%async_computation.1 | async-start | bytes 4718592 | tf_op jit(solution)/shard_map/all_gather | solution.py:30
  356.1 5.4 %copy-start.3 = (f32[512,512]{1,0:T(8,128)S(1)}, f32[512,512]{1,0:T(8,128)}, u32[]{:S(2)}) copy-start(f32[512,512]{1,0:T(8,128)} %param.11) | copy-start | bytes 3145732
  389.9 8.0 %copy-start.1 = (f32[512,512]{1,0:T(8,128)S(1)}, f32[512,512]{1,0:T(8,128)}, u32[]{:S(2)}) copy-start(f32[512,512]{1,0:T(8,128)} %param.10) | copy-start | bytes 3145732
Sparse Core Ops, SparseCore 0:
  14.4 123.0 all-gather.10
  139.2 53.7 all-gather.6
  205.8 117.8 all-gather.12
  325.3 53.7 all-gather.8
